TPU v7x, 32 devices: a whole 2x2x4 slice. The times are simulated.
32 devices in a mesh: arc: 2 (over y), trow: 4 (over z), tcol: 4 (over x, core).
Axes of the slice: x: 2, y: 2, z: 4, core: 2. Of those that a mesh axis runs over, the one named last changes fastest.
Arguments:
- design: bfloat16 [1280, 8192], P('arc', 'tcol'), may hold values from -0.25 to 0.25
- local_design: bfloat16 [1280, 128], P('arc'), may hold values from -0.3125 to 0.3125
- lengths: int32 [4], P('arc'), may hold values from 1 to 320, 960 in all
- regularizer: float32 [8192], P(('arc', 'trow')), may hold values from 0.2 to 2
Outputs:
- normal: float32 [8192, 8192], P(('arc', 'trow'), 'tcol')
- panel_factor: float32 [2, 8192, 512], P(None, 'tcol')
Inputs may be any that keep to these rules, and one draw needn't show every extreme that they name: `lengths`: each arc has at least one live row; some arc is full.
All inputs are finite; a program needn't handle non-finite values. No bound on the sum of `lengths` on one device may be relied on, other than what follows from the above.
Results may differ from a plain program's by a relative error of at most 0.003.
Values may be sent and summed in bfloat16 or wider, within the bound.
No kernel may reach another device: no remote copies, remote signals or barrier semaphores. Data moves between devices by JAX's collectives and lax.ppermute only.
A program may use at most 128 MiB of HBM per device.

v0:
```python
import jax
import jax.numpy as jnp
from jax import lax
from jax.sharding import PartitionSpec as P

PANEL = 512
PANELS = 2


ridge = 0.1


def broadcast(block, axis, holder):
    block = jnp.where(lax.axis_index(axis) == holder, block, jnp.zeros_like(block))
    return lax.psum(block, axis)


def project_arcs(design, local_design, lengths):
    arc_count = lengths.shape[0]
    row_count = design.shape[0]
    capacity = row_count // arc_count
    arc_blocks = design.reshape(arc_count, capacity, design.shape[1])
    local_half = local_design.reshape(arc_count, capacity, local_design.shape[1])
    live_rows = jnp.arange(capacity, dtype=jnp.int32)[None, :] < lengths[:, None]
    arc_blocks = jnp.where(live_rows[:, :, None], arc_blocks, jnp.zeros((), design.dtype))
    local_half = jnp.where(live_rows[:, :, None], local_half, jnp.zeros((), local_design.dtype))
    local_normal = jnp.einsum(
        "acl,acm->alm", local_half, local_half, preferred_element_type=jnp.float32
    )
    local_normal = local_normal + ridge * jnp.eye(local_half.shape[2], dtype=jnp.float32)[None]
    local_factor = jnp.linalg.cholesky(local_normal)
    local_cols = local_half.astype(jnp.float32)
    basis_rows = lax.linalg.triangular_solve(
        local_factor, jnp.transpose(local_cols, (0, 2, 1)), left_side=True, lower=True
    )
    basis_rows = basis_rows.astype(jnp.bfloat16)
    loadings = jnp.einsum(
        "alc,acw->alw", basis_rows, arc_blocks, preferred_element_type=jnp.float32
    ).astype(jnp.bfloat16)
    cleaned = arc_blocks.astype(jnp.float32) - jnp.einsum(
        "alc,alw->acw", basis_rows, loadings, preferred_element_type=jnp.float32
    )
    return cleaned.astype(jnp.bfloat16).reshape(row_count, design.shape[1])


def contract_rows(left_rows, right_rows):
    return lax.dot_general(
        left_rows, right_rows, (((0,), (0,)), ((), ())), preferred_element_type=jnp.float32
    )


def per_device(design, local_design, lengths, regularizer):
    row_count, col_width = design.shape
    tile_rows = regularizer.shape[0]
    arc_total = lax.axis_size("arc")
    trow_total = lax.axis_size("trow")
    trow_index = lax.axis_index("trow")
    row_start = (lax.axis_index("arc") * trow_total + trow_index) * tile_rows
    col_start = lax.axis_index("tcol") * col_width
    projected = project_arcs(design, local_design, lengths)
    gathered = lax.all_gather(projected, "tcol", axis=1, tiled=True)
    regrouped = gathered.reshape(row_count, arc_total, trow_total, tile_rows)
    selected = lax.dynamic_slice_in_dim(regrouped, trow_index, 1, 2).reshape(
        row_count, arc_total * tile_rows
    )
    received = lax.all_to_all(selected, "arc", split_axis=1, concat_axis=0, tiled=True)
    normal_block = contract_rows(received, lax.all_gather(projected, "arc", axis=0, tiled=True))
    rows_global = row_start + jnp.arange(tile_rows, dtype=jnp.int32)
    cols_global = col_start + jnp.arange(col_width, dtype=jnp.int32)
    on_diagonal = rows_global[:, None] == cols_global[None, :]
    normal_block = normal_block + jnp.where(
        on_diagonal, regularizer[:, None], jnp.zeros((), jnp.float32)
    )
    panel_factors = []
    for panel_index in range(PANELS):
        lead_col = panel_index * PANEL
        padded_rows = jnp.pad(normal_block, ((PANEL, PANEL), (0, 0)))
        slice_start = jnp.clip(lead_col - row_start + PANEL, 0, tile_rows + PANEL)
        slice_rows = lax.dynamic_slice_in_dim(padded_rows, slice_start, PANEL, 0)
        panel_global = lead_col + jnp.arange(PANEL, dtype=jnp.int32)
        in_tile = (panel_global >= row_start) & (panel_global < row_start + tile_rows)
        own_share = jnp.where(in_tile[:, None], slice_rows, jnp.zeros((), jnp.float32))
        panel_strip = lax.psum(own_share, ("arc", "trow"))
        pivot_block, row_strip = (
            broadcast(panel_strip[:, lead_col : lead_col + PANEL], "tcol", 0),
            broadcast(normal_block[:, lead_col : lead_col + PANEL], "tcol", 0),
        )
        lower_factor = jnp.linalg.cholesky(pivot_block)
        col_factor = lax.linalg.triangular_solve(
            lower_factor, panel_strip, left_side=True, lower=True
        ).T
        row_factor = lax.linalg.triangular_solve(
            lower_factor, row_strip.T, left_side=True, lower=True
        ).T
        col_factor = jnp.where(
            cols_global[:, None] >= lead_col, col_factor, jnp.zeros((), jnp.float32)
        )
        row_factor = jnp.where(
            rows_global[:, None] >= lead_col, row_factor, jnp.zeros((), jnp.float32)
        )
        normal_block = normal_block - jnp.dot(
            row_factor, col_factor.T, precision=lax.Precision.HIGHEST
        )
        panel_factors.append(col_factor)
    return (normal_block, jnp.stack(panel_factors))


def solution(mesh):
    return jax.shard_map(
        per_device,
        mesh=mesh,
        in_specs=(P("arc", "tcol"), P("arc", None), P("arc"), P(("arc", "trow"))),
        out_specs=(P(("arc", "trow"), "tcol"), P(None, "tcol", None)),
        check_vma=False,
    )
```

profile of v0, /device:TPU:19, one launch (start us, length us, event | category | flops | bytes accessed | tf_op | source)
XLA Modules:
  0.0 1098.5 jit_solution(17169129062626182126)
XLA Ops:
  9.6 23.5 %custom-call.33 = f32[2,128,128]{2,1,0:T(8,128)S(1)} custom-call(f32[2,128,128]{2,1,0:T(8,128)S(1)} %fusion.105), custom_call_target="Cholesky" | custom-call | tf_op jit(solution)/shard_map/jit(cholesky)/cholesky | solution.py:31
  33.4 19.7 %custom-call.34 = f32[2,1,128,128]{2,3,1,0:T(8,128)S(1)} custom-call(f32[2,1,128,128]{3,2,1,0:T(8,128)S(1)} %select_bitcast_fusion), custom_call_target="InvertDiagBlocksLowerTriangular" | custom-call | tf_op jit(solution)/shard_map/triangular_solve | solution.py:33
  54.3 4.0 subtract_convert_fusion
  58.4 3.0 copy.64
  62.1 70.1 %all-gather.3.cloned.1.call-done = bf16[640,8192]{0,1:T(8,128)(2,1)} async-done(((bf16[640,2048]{0,1:T(8,128)(2,1)}), bf16[640,8192]{0,1:T(8,128)(2,1)}) %all-gather.3.cloned.1.call-update) | async-done | bytes 10485776 | tf_op jit(solution)/shard_map/all_gather | solution.py:61
  134.2 2.6 copy.65
  136.8 3.9 all-to-all-start
  141.3 86.7 %all-gather.5.cloned.1.call-done = bf16[1280,2048]{1,0:T(8,128)(2,1)} async-done(((bf16[640,2048]{1,0:T(8,128)(2,1)}), bf16[1280,2048]{1,0:T(8,128)(2,1)}) %all-gather.5.cloned.1.call-update) | async-done | bytes 5242896 | tf_op jit(solution)/shard_map/all_gather | solution.py:67
  228.0 8.0 select_add_fusion
  236.0 3.4 copy-done.1
  239.4 3.2 fusion
  242.7 3.2 fusion.23
  245.9 152.0 %all-reduce.10.cloned.1.call-done = f32[512,2048]{0,1:T(8,128)} async-done(((f32[512,2048]{0,1:T(8,128)}), f32[512,2048]{0,1:T(8,128)}) %all-reduce.10.cloned.1.call-update) | async-done | bytes 4194320 | tf_op jit(solution)/shard_map/psum | solution.py:83
  400.3 68.2 %all-reduce.16.cloned.1.call-done = (f32[512,512]{0,1:T(8,128)}, f32[512,1024]{1,0:T(8,128)}) async-done(((f32[512,512]{0,1:T(8,128)}, f32[512,1024]{1,0:T(8,128)}), (f32[512,512]{0,1:T(8,128)}, f32[512,1024]{1,0:T(8,128)})) %all-reduce.16.cloned.1.call-update) | async-done | bytes 3145744 | tf_op jit(solution)/shard_map/psum | solution.py:15
  471.6 11.7 %cholesky.327 = f32[128,128]{1,0:T(8,128)S(1)} custom-call(f32[128,128]{1,0:T(8,128)S(1)} %cholesky.467), custom_call_target="Cholesky" | custom-call | tf_op jit(solution)/shard_map/jit(cholesky)/cholesky | solution.py:88
  483.4 9.8 custom-call.40
  493.9 11.7 %cholesky.346 = f32[128,128]{1,0:T(8,128)S(1)} custom-call(f32[128,128]{1,0:T(8,128)S(1)} %cholesky.471), custom_call_target="Cholesky" | custom-call | tf_op jit(solution)/shard_map/jit(cholesky)/cholesky | solution.py:88
  505.7 10.0 custom-call.41
  516.3 11.7 %cholesky.367 = f32[128,128]{1,0:T(8,128)S(1)} custom-call(f32[128,128]{1,0:T(8,128)S(1)} %cholesky.476), custom_call_target="Cholesky" | custom-call | tf_op jit(solution)/shard_map/jit(cholesky)/cholesky | solution.py:88
  528.0 9.8 custom-call.42
  538.5 11.7 %cholesky.384 = f32[128,128]{1,0:T(8,128)S(1)} custom-call(f32[128,128]{1,0:T(8,128)S(1)} %convolution_subtract_fusion.15), custom_call_target="Cholesky" | custom-call | tf_op jit(solution)/shard_map/jit(cholesky)/cholesky | solution.py:88
  555.9 7.7 while.8
  563.6 39.3 %custom-call.43 = f32[4,128,128]{1,2,0:T(8,128)S(1)} custom-call(f32[4,128,128]{2,1,0:T(8,128)S(1)} %get-tuple-element.33), custom_call_target="InvertDiagBlocksLowerTriangular" | custom-call | tf_op jit(solution)/shard_map/triangular_solve/custom-call.9 | solution.py:92
  605.6 3.0 convolution_subtract_fusion.5
  611.1 4.8 convolution_subtract_fusion.3
  620.6 7.3 fusion.17
  636.8 15.1 %convolution_subtract_fusion.1 = f32[1024,2048]{0,1:T(8,128)S(1)} fusion(f32[1024,2048]{0,1:T(8,128)S(1)} %bitcast.164, f32[128,2048]{0,1:T(8,128)S(1)} %fusion.128, f32[128,2048]{0,1:T(8,128)S(1)} %copy-done.4, f32[128,2048]{0,1:T(8,128)S(1)} %copy-done.3, f32[128,2048]{0,1:T(8,128)S(1)} %copy.71, f32[128,1024]{1,0:T(8,128)S(1)} %fusion.129, ...), kind=kOutput, calls=%fused_computation.14 | convolution fusion | flops 12893290496 | bytes 23071744 | tf_op jit(solution)/shard_map/dot_general | solution.py:101
  651.9 3.4 copy-done
  655.3 3.2 fusion.1
  658.5 3.2 fusion.22
  661.7 153.1 %all-reduce.12.cloned.1.call-done = f32[512,2048]{0,1:T(8,128)} async-done(((f32[512,2048]{0,1:T(8,128)}), f32[512,2048]{0,1:T(8,128)}) %all-reduce.12.cloned.1.call-update) | async-done | bytes 4194320 | tf_op jit(solution)/shard_map/psum | solution.py:83
  817.2 3.6 fusion.21
  820.8 64.7 %all-reduce.14.cloned.1.call-done = (f32[512,512]{0,1:T(8,128)}, f32[512,1024]{1,0:T(8,128)}) async-done(((f32[512,512]{0,1:T(8,128)}, f32[512,1024]{1,0:T(8,128)}), (f32[512,512]{0,1:T(8,128)}, f32[512,1024]{1,0:T(8,128)})) %all-reduce.14.cloned.1.call-update) | async-done | bytes 3145744 | tf_op jit(solution)/shard_map/psum | solution.py:15
  888.5 11.7 %cholesky.399 = f32[128,128]{1,0:T(8,128)S(1)} custom-call(f32[128,128]{1,0:T(8,128)S(1)} %cholesky.480), custom_call_target="Cholesky" | custom-call | tf_op jit(solution)/shard_map/jit(cholesky)/cholesky | solution.py:88
  900.4 9.8 custom-call.45
  910.9 11.7 %cholesky.418 = f32[128,128]{1,0:T(8,128)S(1)} custom-call(f32[128,128]{1,0:T(8,128)S(1)} %cholesky.484), custom_call_target="Cholesky" | custom-call | tf_op jit(solution)/shard_map/jit(cholesky)/cholesky | solution.py:88
  922.6 10.0 custom-call.46
  933.2 11.7 %cholesky.439 = f32[128,128]{1,0:T(8,128)S(1)} custom-call(f32[128,128]{1,0:T(8,128)S(1)} %cholesky.489), custom_call_target="Cholesky" | custom-call | tf_op jit(solution)/shard_map/jit(cholesky)/cholesky | solution.py:88
  945.0 9.8 custom-call.47
  955.4 11.7 %cholesky.456 = f32[128,128]{1,0:T(8,128)S(1)} custom-call(f32[128,128]{1,0:T(8,128)S(1)} %convolution_subtract_fusion.14), custom_call_target="Cholesky" | custom-call | tf_op jit(solution)/shard_map/jit(cholesky)/cholesky | solution.py:88
  972.7 8.3 while.9
  981.0 39.3 %custom-call.48 = f32[4,128,128]{1,2,0:T(8,128)S(1)} custom-call(f32[4,128,128]{2,1,0:T(8,128)S(1)} %get-tuple-element.35), custom_call_target="InvertDiagBlocksLowerTriangular" | custom-call | tf_op jit(solution)/shard_map/triangular_solve/custom-call.9 | solution.py:92
  1023.0 3.0 convolution_subtract_fusion.4
  1028.4 4.8 convolution_subtract_fusion.2
  1037.9 7.5 fusion.14
  1058.1 16.5 %convolution_subtract_fusion = f32[1024,2048]{0,1:T(8,128)} fusion(f32[1024,2048]{0,1:T(8,128)S(1)} %bitcast.162, f32[128,2048]{0,1:T(8,128)S(1)} %fusion.134, f32[128,2048]{0,1:T(8,128)S(1)} %copy-done.7, f32[128,2048]{0,1:T(8,128)S(1)} %copy-done.6, f32[128,2048]{0,1:T(8,128)S(1)} %copy.80, f32[128,1024]{1,0:T(8,128)S(1)} %fusion.135, ...), kind=kOutput, calls=%fused_computation.13 | convolution fusion | flops 12893290496 | bytes 23071744 | tf_op jit(solution)/shard_map/dot_general | solution.py:101
  1074.5 9.1 copy.85
  1083.7 7.8 pad_maximum_fusion
  (168 shorter events, 85.0 us)
Async XLA Ops:
  7.2 125.1 %all-gather.3.cloned.1.call-start = ((), (), s32[]{:S(2)}) async-start(), calls=%async_computation.1 | async-start | bytes 13107200 | tf_op jit(solution)/shard_map/all_gather | solution.py:61
  58.4 3.1 copy-start.2
  61.4 166.6 %all-gather.5.cloned.1.call-start = ((), (), s32[]{:S(2)}) async-start(), calls=%async_computation.2 | async-start | bytes 7864320 | tf_op jit(solution)/shard_map/all_gather | solution.py:67
  134.2 93.8 %copy-start.12 = (f32[1024]{0:T(1024)S(1)}, f32[1024]{0:T(1024)}, u32[]{:S(2)}) copy-start(f32[1024]{0:T(1024)} %param.12) | copy-start | bytes 12292
  136.8 91.1 %all-to-all-start = ((bf16[640,2,1024]{2,0,1:T(8,128)(2,1)}), bf16[640,2,1024]{2,0,1:T(8,128)(2,1)S(1)}, u32[]{:S(2)}, u32[]{:S(2)}) async-start(bf16[640,2,1024]{2,0,1:T(8,128)(2,1)} %bitcast.7), calls=%async_computation | async-start | bytes 5242880 | tf_op jit(solution)/shard_map/all_to_all | solution.py:66
  140.7 257.2 %all-reduce.10.cloned.1.call-start = ((), (), s32[]{:S(2)}) async-start(), calls=%async_computation.3 | async-start | bytes 8388608 | tf_op jit(solution)/shard_map/psum | solution.py:83
  236.0 3.4 copy-start.1
  242.6 225.9 %all-reduce.16.cloned.1.call-start = ((), (), s32[]{:S(2)}) async-start(), calls=%async_computation.6 | async-start | bytes 6291456 | tf_op jit(solution)/shard_map/psum | solution.py:15
  400.2 414.6 %all-reduce.12.cloned.1.call-start = ((), (), s32[]{:S(2)}) async-start(), calls=%async_computation.4 | async-start | bytes 8388608 | tf_op jit(solution)/shard_map/psum | solution.py:83
  563.6 42.0 %copy-start.9 = (f32[512,512]{1,0:T(8,128)}, f32[512,512]{1,0:T(8,128)S(1)}, u32[]{:S(2)}) copy-start(f32[512,512]{1,0:T(8,128)S(1)} %get-tuple-element.210) | copy-start | bytes 3145732
  620.6 8.3 copy-start.10
  620.6 16.2 %slice-start.2 = ((s8[8388608]{0:T(1024)(128)(4,1)}), s8[4194304]{0:T(1024)(128)(4,1)S(1)}, s32[]{:S(2)}) async-start(s8[8388608]{0:T(1024)(128)(4,1)} %bitcast.163), calls=%async_computation.9 | async-start | bytes 8388608
  628.9 7.9 copy-start.5
  629.5 7.2 slice-start.3
  631.1 5.7 copy-start.3
  631.1 5.7 copy-start.4
  651.9 3.4 copy-start
  658.5 227.0 %all-reduce.14.cloned.1.call-start = ((), (), s32[]{:S(2)}) async-start(), calls=%async_computation.5 | async-start | bytes 6291456 | tf_op jit(solution)/shard_map/psum | solution.py:15
  981.0 42.0 %copy-start.8 = (f32[512,512]{1,0:T(8,128)}, f32[512,512]{1,0:T(8,128)S(1)}, u32[]{:S(2)}) copy-start(f32[512,512]{1,0:T(8,128)S(1)} %get-tuple-element.209) | copy-start | bytes 3145732
  1037.9 8.6 copy-start.11
  1048.5 5.8 copy-start.6
  1048.6 5.8 copy-start.7
  1049.2 7.5 slice-start
  1054.3 3.7 slice-start.1
Sparse Core Ops, SparseCore 0:
  61.5 70.7 all-gather.2
  134.4 93.5 all-gather.4
  242.7 155.1 all-reduce.9
  400.7 67.7 all-reduce.15
  658.6 156.1 all-reduce.11
  817.7 67.7 all-reduce.13
where the time goes:
time: 1110 us; the launch traced here: 1100 us
  waiting for transfers between devices  596 us (54%)
  other arithmetic  316 us (28%)
  matrix products  109 us (10%)
  local copies, waits for them, and re-layouts  52.6 us (5%)
  between operations  20.3 us (2%)
    psum x2, waiting for transfers between devices, per_device(): panel_strip = lax.psum(own_share, ('arc', 'trow'))  305 us
    another operation x30, other arithmetic, per_device(): lower_factor = jnp.linalg.cholesky(pivot_block)  158 us
    psum x2, waiting for transfers between devices, broadcast(): return lax.psum(block, axis)  133 us
    all_gather x1, waiting for transfers between devices, per_device(): lax.all_gather(projected, 'arc', axis=0, tiled=True)  86.7 us
    another operation x5, other arithmetic, per_device(): lax.linalg.triangular_solve(lower_factor, row_strip.T, left_side=True, lo...  79.5 us
    all_gather x1, waiting for transfers between devices, per_device(): gathered = lax.all_gather(projected, 'tcol', axis=1, tiled=True)  70.1 us
    another operation x14, matrix products, per_device(): lax.linalg.triangular_solve(lower_factor, panel_strip, left_side=True, lo...  43.5 us
    dot_general x2, matrix products, per_device(): jnp.dot(row_factor, col_factor.T, precision=lax.Precision.HIGHEST)  31.6 us
  transfers between devices with their start and end apart: 7, of which 6 were waited for; matrix products, arithmetic and copies ran while one was open for 1% of the time, Pallas kernels for 0%

commit v1 on v0

v1 whole, which is shorter than its diff:
```python
import jax
import jax.numpy as jnp
from jax import lax
from jax.sharding import PartitionSpec as P

PANEL = 512
PANELS = 2
AXES = ("arc", "trow", "tcol")

ridge = 0.1

HIGHEST = lax.Precision.HIGHEST


class Plan:
    def __init__(self, mesh):
        self.arc, self.trow, self.tcol = (mesh.shape[name] for name in AXES)

    def flat(self, arc, trow, tcol):
        return (arc * self.trow + trow) * self.tcol + tcol

    def devices(self):
        for arc in range(self.arc):
            for trow in range(self.trow):
                for tcol in range(self.tcol):
                    yield arc, trow, tcol

    def shift_arc(self, block, step, keep=None):
        pairs = [
            (self.flat(a, r, c), self.flat((a + step) % self.arc, r, c))
            for a, r, c in self.devices()
            if keep is None or keep(a, r, c)
        ]
        return lax.ppermute(block, AXES, pairs)

    def gather_arc(self, block, keep=None):
        return [block] + [self.shift_arc(block, s, keep) for s in range(1, self.arc)]

    def spread_tcol(self, block, holder):
        me = lax.axis_index("tcol")
        offsets = [0]
        index = lax.axis_index("arc") * self.trow + lax.axis_index("trow")
        table = jnp.array(
            [holder(a, r) for a in range(self.arc) for r in range(self.trow)], jnp.int32
        )
        offset = me ^ table[index]
        span = self.tcol // 2
        while span:
            pairs = [
                (self.flat(a, r, holder(a, r) ^ o), self.flat(a, r, holder(a, r) ^ o ^ span))
                for a in range(self.arc)
                for r in range(self.trow)
                for o in offsets
            ]
            got = lax.ppermute(block, AXES, pairs)
            received = (offset & (2 * span - 1)) == span
            block = jnp.where(received, got, block)
            offsets = offsets + [o ^ span for o in offsets]
            span //= 2
        return block

    def order_arcs(self, pieces):
        stacked = jnp.stack(pieces)
        if self.arc == 1:
            return stacked
        me = lax.axis_index("arc")
        return jnp.take(stacked, (me - jnp.arange(self.arc)) % self.arc, axis=0)

    def gather_rows(self, tile):
        me = lax.axis_index("arc") * self.trow + lax.axis_index("trow")
        total = self.arc * self.trow
        span = 1
        while span < total:
            pairs = [
                (self.flat(a, r, c), self.flat((t ^ span) // self.trow, (t ^ span) % self.trow, c))
                for a, r, c in self.devices()
                for t in [a * self.trow + r]
            ]
            got = lax.ppermute(tile, AXES, pairs)
            low = (me & span) == 0
            tile = jnp.concatenate([jnp.where(low, tile, got), jnp.where(low, got, tile)])
            span *= 2
        return tile


def local_basis(local_half):
    local_normal = jnp.einsum(
        "acl,acm->alm", local_half, local_half, preferred_element_type=jnp.float32
    )
    local_normal = local_normal + ridge * jnp.eye(local_half.shape[2], dtype=jnp.float32)[None]
    local_factor = jnp.linalg.cholesky(local_normal)
    local_cols = local_half.astype(jnp.float32)
    basis_rows = lax.linalg.triangular_solve(
        local_factor, jnp.transpose(local_cols, (0, 2, 1)), left_side=True, lower=True
    )
    return basis_rows.astype(jnp.bfloat16)


def project(blocks, basis):
    loadings = jnp.einsum(
        "alc,acw->alw", basis, blocks, preferred_element_type=jnp.float32
    ).astype(jnp.bfloat16)
    cleaned = blocks.astype(jnp.float32) - jnp.einsum(
        "alc,alw->acw", basis, loadings, preferred_element_type=jnp.float32
    )
    cleaned = cleaned.astype(jnp.bfloat16)
    return cleaned.reshape(-1, cleaned.shape[2])


def contract_rows(left_rows, right_rows):
    return lax.dot_general(
        left_rows, right_rows, (((0,), (0,)), ((), ())), preferred_element_type=jnp.float32
    )


def per_device(plan, design, local_design, lengths, regularizer):
    row_count, col_width = design.shape
    tile_rows = regularizer.shape[0]
    own_arcs = lengths.shape[0]
    capacity = row_count // own_arcs
    tile_index = lax.axis_index("arc") * plan.trow + lax.axis_index("trow")
    row_start = tile_index * tile_rows
    col_start = lax.axis_index("tcol") * col_width
    lead = PANEL * PANELS

    live_rows = jnp.arange(capacity, dtype=jnp.int32)[None, :] < lengths[:, None]
    live_flat = live_rows.reshape(row_count, 1)
    masked = jnp.where(live_flat, design, jnp.zeros((), design.dtype))
    local_half = local_design.reshape(own_arcs, capacity, -1)
    local_half = jnp.where(live_rows[:, :, None], local_half, jnp.zeros((), local_design.dtype))

    lead_own = masked[:, :lead]
    lead_pieces = [
        plan.spread_tcol(piece, lambda a, r: 0)
        for piece in plan.gather_arc(lead_own, lambda a, r, c: c == 0)
    ]
    col_pieces = plan.gather_arc(masked)

    def tile_holder(a, r):
        return (a * plan.trow + r) * tile_rows // col_width

    tile_offset = lax.rem(row_start, col_width)
    row_pieces = [
        plan.spread_tcol(
            lax.dynamic_slice_in_dim(piece, tile_offset, tile_rows, 1), tile_holder
        )
        for piece in col_pieces
    ]
    all_regularizer = plan.gather_rows(regularizer)

    basis_own = local_basis(local_half)
    basis = plan.order_arcs(plan.gather_arc(basis_own)).reshape(-1, *basis_own.shape[1:])

    def whole(pieces):
        blocks = plan.order_arcs(pieces)
        return blocks.reshape(-1, capacity, blocks.shape[-1])

    lead_rows = project(whole(lead_pieces), basis)
    pivot = contract_rows(lead_rows, lead_rows) + jnp.diag(all_regularizer[:lead])

    cols_global = col_start + jnp.arange(col_width, dtype=jnp.int32)
    rows_global = row_start + jnp.arange(tile_rows, dtype=jnp.int32)
    both_global = jnp.concatenate([cols_global, rows_global])
    col_rows = project(whole(col_pieces), basis)
    tile_cols = project(whole(row_pieces), basis)
    both = jnp.concatenate([col_rows, tile_cols], axis=1)
    strips = contract_rows(lead_rows, both)
    lead_ids = jnp.arange(lead, dtype=jnp.int32)
    strips = strips + jnp.where(
        lead_ids[:, None] == both_global[None, :],
        all_regularizer[:lead, None],
        jnp.zeros((), jnp.float32),
    )
    normal_block = contract_rows(tile_cols, col_rows)
    normal_block = normal_block + jnp.where(
        rows_global[:, None] == cols_global[None, :],
        regularizer[:, None],
        jnp.zeros((), jnp.float32),
    )
    panel_factors = []
    for panel in range(PANELS):
        lower = jnp.linalg.cholesky(pivot[:PANEL, :PANEL])
        wide = jnp.concatenate([pivot[:PANEL, PANEL:], strips[:PANEL]], axis=1)
        solved = lax.linalg.triangular_solve(lower, wide, left_side=True, lower=True)
        left = pivot.shape[1] - PANEL
        ahead, factor = solved[:, :left], solved[:, left:]
        factor = jnp.where(
            both_global[None, :] >= panel * PANEL, factor, jnp.zeros((), jnp.float32)
        )
        panel_factors.append(factor)
        if left:
            pivot = pivot[PANEL:, PANEL:] - lax.dot_general(
                ahead, ahead, (((0,), (0,)), ((), ())), precision=HIGHEST
            )
            strips = strips[PANEL:] - lax.dot_general(
                ahead, factor, (((0,), (0,)), ((), ())), precision=HIGHEST
            )
    stacked = jnp.concatenate(panel_factors)
    normal_block = normal_block - lax.dot_general(
        stacked[:, col_width:],
        stacked[:, :col_width],
        (((0,), (0,)), ((), ())),
        precision=HIGHEST,
    )
    outs = jnp.stack([jnp.transpose(f[:, :col_width]) for f in panel_factors])
    return (normal_block, outs)


def solution(mesh):
    plan = Plan(mesh)

    def body(*args):
        return per_device(plan, *args)

    return jax.shard_map(
        body,
        mesh=mesh,
        in_specs=(P("arc", "tcol"), P("arc", None), P("arc"), P(("arc", "trow"))),
        out_specs=(P(("arc", "trow"), "tcol"), P(None, "tcol", None)),
        check_vma=False,
    )
```

time: 1110 us -> 582 us (0.52)
  waiting for transfers between devices: 596 us -> 16.4 us
  matrix products: 109 us -> 134 us
  starting transfers between devices: 4.57 us -> 28.9 us
  between operations: 20.3 us -> 7.47 us
  other arithmetic: 316 us -> 328 us
    psum x4 -> x0, waiting for transfers between devices: 438 us -> none  [the longest x2 305 us: per_device(): panel_strip = lax.psum(own_share, ('arc', 'trow'))]
    all_gather x2 -> x0, waiting for transfers between devices: 157 us -> none  [the longest x1 86.7 us: per_device(): lax.all_gather(projected, 'arc', axis=0, tiled=True)]
    ppermute x0 -> x14, starting transfers between devices: none -> 28.9 us  [the longest x8 21 us: spread_tcol(): got = lax.ppermute(block, AXES, pairs)]
    dot_general x4 -> x7, matrix products: 37.1 us -> 64.6 us  [the longest x1 31.3 us: per_device(): lax.dot_general(stacked[:, col_width:], stacked[:, :col_width], (((0,), (...]
    another operation x41 -> x27, matrix products: 64.1 us -> 38 us  [the longest x14 33.9 us: per_device(): lax.linalg.triangular_solve(lower, wide, left_side=True, lower=True)]
    dot_general x1 -> x3, matrix products: 8.04 us -> 31.5 us  [contract_rows(): lax.dot_general(left_rows, right_rows, (((0,), (0,)), ((), ())), preferre...]
    ppermute x0 -> x14, waiting for transfers between devices: none -> 16.4 us  [the longest x8 16.2 us: spread_tcol(): got = lax.ppermute(block, AXES, pairs)]
    gather x0 -> x5, local copies, waits for them, and re-layouts: none -> 11.2 us  [order_arcs(): return jnp.take(stacked, (me - jnp.arange(self.arc)) % self.arc, axis=0)]
  transfers between devices with their start and end apart: 7 -> 14, of which waited for: 6 -> 2; matrix products, arithmetic and copies ran while one was open for 1% -> 17% of each run, Pallas kernels for 0% -> 0%
where the time goes in v1:
time: 582 us; the launch traced here: 571 us
  other arithmetic  328 us (56%)
  matrix products  134 us (23%)
  local copies, waits for them, and re-layouts  55.8 us (10%)
  starting transfers between devices  28.9 us (5%)
  waiting for transfers between devices  16.4 us (3%)
  between operations  7.47 us (1%)
    another operation x30, other arithmetic, per_device(): lower = jnp.linalg.cholesky(pivot[:PANEL, :PANEL])  159 us
    another operation x6, other arithmetic, per_device(): lax.linalg.triangular_solve(lower, wide, left_side=True, lower=True)  80.2 us
    another operation x14, matrix products, per_device(): lax.linalg.triangular_solve(lower, wide, left_side=True, lower=True)  33.9 us
    dot_general x3, matrix products, contract_rows(): lax.dot_general(left_rows, right_rows, (((0,), (0,)), ((), ())), preferre...  31.5 us
    dot_general x1, matrix products, per_device(): lax.dot_general(stacked[:, col_width:], stacked[:, :col_width], (((0,), (...  31.3 us
    another operation x4, other arithmetic, local_basis(): local_factor = jnp.linalg.cholesky(local_normal)  23.6 us
    ppermute x8, starting transfers between devices, spread_tcol(): got = lax.ppermute(block, AXES, pairs)  21 us
    another operation x3, other arithmetic, local_basis(): lax.linalg.triangular_solve(local_factor, jnp.transpose(local_cols, (0, 2...  19.8 us
  transfers between devices with their start and end apart: 14, of which 2 were waited for; matrix products, arithmetic and copies ran while one was open for 17% of the time, Pallas kernels for 0%

profile of v1, /device:TPU:19, one launch (start us, length us, event | category | flops | bytes accessed | tf_op | source)
XLA Modules:
  0.0 570.8 jit_solution(18317725701417857673)
XLA Ops:
  10.3 23.5 %custom-call.33 = f32[2,128,128]{2,1,0:T(8,128)S(1)} custom-call(f32[2,128,128]{2,1,0:T(8,128)S(1)} %fusion.64), custom_call_target="Cholesky" | custom-call | tf_op jit(solution)/shard_map/jit(cholesky)/cholesky | solution.py:91
  34.0 19.7 %custom-call.34 = f32[2,1,128,128]{2,3,1,0:T(8,128)S(1)} custom-call(f32[2,1,128,128]{3,2,1,0:T(8,128)S(1)} %select_bitcast_fusion.4), custom_call_target="InvertDiagBlocksLowerTriangular" | custom-call | tf_op jit(solution)/shard_map/triangular_solve | solution.py:93
  56.9 3.5 fusion.130
  65.9 3.2 collective-permute-start.13
  80.8 16.2 %collective-permute-done = bf16[640,1024]{1,0:T(8,128)(2,1)} collective-permute-done((bf16[640,1024]{1,0:T(8,128)(2,1)}, bf16[640,1024]{1,0:T(8,128)(2,1)}, u32[]{:S(2)}, u32[]{:S(2)}) %collective-permute-start) | collective-permute-done | bytes 1310752 | tf_op jit(solution)/shard_map/ppermute | solution.py:55
  99.5 9.9 %collective-permute-start.1 = (bf16[640,1024]{1,0:T(8,128)(2,1)}, bf16[640,1024]{1,0:T(8,128)(2,1)}, u32[]{:S(2)}, u32[]{:S(2)}) collective-permute-start(bf16[640,1024]{1,0:T(8,128)(2,1)} %broadcast_select_fusion.9), channel_id=1, source_target_pairs={{0,1},{2,3},{4,5},{6,7},{9,8},{11,10},{13,12},{15,14},{18,19},{16,... | collective-permute-start | bytes 3932168 | tf_op jit(solution)/shard_map/ppermute | solution.py:55
  109.3 3.1 fusion.32
  112.4 4.0 gather_fusion.1
  118.6 5.6 pad_maximum_fusion.4
  124.2 3.3 broadcast_select_fusion.8
  129.9 9.2 %subtract_convert_fusion = bf16[4,320,2048]{2,1,0:T(8,128)(2,1)} fusion(bf16[4,128,320]{1,2,0:T(8,128)(2,1)S(1)} %bitcast_select_fusion, bf16[4,320,2048]{2,1,0:T(8,128)(2,1)} %bitcast.171, pred[4]{0:T(512)(128)(4,1)S(1)} %broadcast_in_dim.137), kind=kOutput, calls=%fused_computation.14 | convolution fusion | flops 1356333056 | bytes 10813444 | tf_op jit(solution)/shard_map/alc,alw->acw/dot_general | solution.py:103
  149.9 4.6 broadcast_select_fusion.2
  154.5 2.9 subtract_convert_fusion.1
  157.4 5.6 bitcast_add_fusion.1
  167.2 11.7 %cholesky.327 = f32[128,128]{1,0:T(8,128)S(1)} custom-call(f32[128,128]{1,0:T(8,128)S(1)} %cholesky.467), custom_call_target="Cholesky" | custom-call | tf_op jit(solution)/shard_map/jit(cholesky)/cholesky | solution.py:182
  179.1 9.9 %custom-call.40 = f32[1,128,128]{1,2,0:T(8,128)S(1)} custom-call(f32[1,128,128]{2,1,0:T(8,128)S(1)} %get-tuple-element.69), custom_call_target="InvertDiagBlocksLowerTriangular" | custom-call | tf_op jit(solution)/shard_map/jit(cholesky)/cholesky | solution.py:182
  189.7 11.7 %cholesky.346 = f32[128,128]{1,0:T(8,128)S(1)} custom-call(f32[128,128]{1,0:T(8,128)S(1)} %cholesky.471), custom_call_target="Cholesky" | custom-call | tf_op jit(solution)/shard_map/jit(cholesky)/cholesky | solution.py:182
  202.7 9.8 %custom-call.41 = f32[1,128,128]{1,2,0:T(8,128)S(1)} custom-call(f32[1,128,128]{2,1,0:T(8,128)S(1)} %get-tuple-element.66), custom_call_target="InvertDiagBlocksLowerTriangular" | custom-call | tf_op jit(solution)/shard_map/jit(cholesky)/cholesky | solution.py:182
  213.1 11.7 %cholesky.367 = f32[128,128]{1,0:T(8,128)S(1)} custom-call(f32[128,128]{1,0:T(8,128)S(1)} %cholesky.476), custom_call_target="Cholesky" | custom-call | tf_op jit(solution)/shard_map/jit(cholesky)/cholesky | solution.py:182
  225.6 10.0 %custom-call.42 = f32[1,128,128]{1,2,0:T(8,128)S(1)} custom-call(f32[1,128,128]{2,1,0:T(8,128)S(1)} %get-tuple-element.63), custom_call_target="InvertDiagBlocksLowerTriangular" | custom-call | tf_op jit(solution)/shard_map/jit(cholesky)/cholesky | solution.py:182
  236.2 11.7 %cholesky.384 = f32[128,128]{1,0:T(8,128)S(1)} custom-call(f32[128,128]{1,0:T(8,128)S(1)} %convolution_subtract_fusion.7), custom_call_target="Cholesky" | custom-call | tf_op jit(solution)/shard_map/jit(cholesky)/cholesky | solution.py:182
  251.2 7.2 %while.2 = (s32[]{:T(128)}, f32[512,512]{1,0:T(8,128)S(1)}, s32[4,2]{0,1:T(2,128)S(1)}, f32[4,128,128]{2,1,0:T(8,128)S(1)}, s32[]{:T(128)}) while((s32[]{:T(128)}, f32[512,512]{1,0:T(8,128)S(1)}, s32[4,2]{0,1:T(2,128)S(1)}, f32[4,128,128]{2,1,0:T(8,128)S(1)}, s32[]{:T(128)}) %tuple.63), condition=%wide.while_cond, body=%wide.while_body.sunk | while | flops 2 | bytes 131181 | solution.py:184
  258.5 39.7 %custom-call.35 = f32[4,128,128]{1,2,0:T(8,128)S(1)} custom-call(f32[4,128,128]{2,1,0:T(8,128)S(1)} %get-tuple-element.11), custom_call_target="InvertDiagBlocksLowerTriangular" | custom-call | tf_op jit(solution)/shard_map/triangular_solve | solution.py:184
  298.2 4.0 subtract_convert_fusion.2
  302.2 13.6 %select_add_fusion = f32[1024,3072]{1,0:T(8,128)S(1)} fusion(f32[1024]{0:T(1024)S(1)} %copy-done.16, s32[3072]{0:T(1024)S(1)} %copy-done.14, bf16[1280,1024]{1,0:T(8,128)(2,1)} %bitcast.173, bf16[1280,1024]{1,0:T(8,128)(2,1)S(1)} %bitcast.168, bf16[1280,2048]{1,0:T(8,128)(2,1)} %bitcast.172), kind=kOutput, calls=%fused_computation.12 | convolution fusion | flops 8078229504 | bytes 23085056 | tf_op jit(solution)/shard_map/dot_general | solution.py:111
  315.9 3.3 slice.203
  319.2 3.1 copy-done.1
  324.1 3.4 fusion.35
  331.8 3.0 convolution_subtract_fusion
  336.6 4.4 fusion.13
  343.6 3.4 slice_subtract_fusion.7
  349.2 12.9 %slice_subtract_fusion = f32[512,3072]{1,0:T(8,128)} fusion(f32[1024,3072]{1,0:T(8,128)S(1)} %bitcast.167, f32[512,512]{1,0:T(8,128)S(1)} %pad_maximum_fusion.9, f32[512,3072]{1,0:T(8,128)S(1)} %slice_select_fusion), kind=kOutput, calls=%fused_computation.29 | convolution fusion | flops 9665249280 | bytes 19922944 | tf_op jit(solution)/shard_map/dot_general | solution.py:195
  365.0 11.7 %cholesky.399 = f32[128,128]{1,0:T(8,128)S(1)} custom-call(f32[128,128]{1,0:T(8,128)S(1)} %cholesky.480), custom_call_target="Cholesky" | custom-call | tf_op jit(solution)/shard_map/jit(cholesky)/cholesky | solution.py:182
  376.8 9.8 %custom-call.43 = f32[1,128,128]{1,2,0:T(8,128)S(1)} custom-call(f32[1,128,128]{2,1,0:T(8,128)S(1)} %get-tuple-element.59), custom_call_target="InvertDiagBlocksLowerTriangular" | custom-call | tf_op jit(solution)/shard_map/jit(cholesky)/cholesky | solution.py:182
  387.3 11.7 %cholesky.418 = f32[128,128]{1,0:T(8,128)S(1)} custom-call(f32[128,128]{1,0:T(8,128)S(1)} %cholesky.484), custom_call_target="Cholesky" | custom-call | tf_op jit(solution)/shard_map/jit(cholesky)/cholesky | solution.py:182
  400.4 9.9 %custom-call.44 = f32[1,128,128]{1,2,0:T(8,128)S(1)} custom-call(f32[1,128,128]{2,1,0:T(8,128)S(1)} %get-tuple-element.56), custom_call_target="InvertDiagBlocksLowerTriangular" | custom-call | tf_op jit(solution)/shard_map/jit(cholesky)/cholesky | solution.py:182
  411.0 11.7 %cholesky.439 = f32[128,128]{1,0:T(8,128)S(1)} custom-call(f32[128,128]{1,0:T(8,128)S(1)} %cholesky.489), custom_call_target="Cholesky" | custom-call | tf_op jit(solution)/shard_map/jit(cholesky)/cholesky | solution.py:182
  423.4 9.8 %custom-call.45 = f32[1,128,128]{1,2,0:T(8,128)S(1)} custom-call(f32[1,128,128]{2,1,0:T(8,128)S(1)} %get-tuple-element.53), custom_call_target="InvertDiagBlocksLowerTriangular" | custom-call | tf_op jit(solution)/shard_map/jit(cholesky)/cholesky | solution.py:182
  433.9 11.7 %cholesky.456 = f32[128,128]{1,0:T(8,128)S(1)} custom-call(f32[128,128]{1,0:T(8,128)S(1)} %convolution_subtract_fusion.6), custom_call_target="Cholesky" | custom-call | tf_op jit(solution)/shard_map/jit(cholesky)/cholesky | solution.py:182
  448.8 8.1 %while.3 = (s32[]{:T(128)}, f32[512,512]{1,0:T(8,128)S(1)}, s32[4,2]{0,1:T(2,128)S(1)}, f32[4,128,128]{2,1,0:T(8,128)S(1)}, s32[]{:T(128)}) while((s32[]{:T(128)}, f32[512,512]{1,0:T(8,128)S(1)}, s32[4,2]{0,1:T(2,128)S(1)}, f32[4,128,128]{2,1,0:T(8,128)S(1)}, s32[]{:T(128)}) %tuple.69), condition=%wide.while_cond.1, body=%wide.while_body.1.sunk | while | flops 2 | bytes 131181 | solution.py:184
  457.0 39.7 %custom-call.36 = f32[4,128,128]{1,2,0:T(8,128)S(1)} custom-call(f32[4,128,128]{2,1,0:T(8,128)S(1)} %get-tuple-element.19), custom_call_target="InvertDiagBlocksLowerTriangular" | custom-call | tf_op jit(solution)/shard_map/triangular_solve | solution.py:184
  496.7 2.9 fusion.41
  501.1 3.1 fusion.40
  507.5 2.9 fusion.16
  513.7 31.3 %fusion = f32[1024,2048]{1,0:T(8,128)} fusion(f32[512,3072]{1,0:T(8,128)S(1)} %maximum_select_fusion, f32[512,3072]{1,0:T(8,128)S(1)} %bitcast.163), kind=kOutput, calls=%fused_computation.16 | convolution fusion | flops 25772949504 | bytes 20971520 | tf_op jit(solution)/shard_map/dot_general | solution.py:199
  545.1 4.3 pad_maximum_fusion.2
  549.4 8.8 %copy.23 = f32[2,2048,512]{2,1,0:T(8,128)} copy(f32[2,2048,512]{1,2,0:T(8,128)} %pad_maximum_fusion.2) | data formatting | bytes 16777216
  558.2 12.3 %fusion.2 = f32[1024,2048]{1,0:T(8,128)} fusion(f32[1024,2048]{1,0:T(8,128)} %fusion, bf16[4,320,1024]{2,1,0:T(8,128)(2,1)S(1)} %copy-done.4, bf16[4,320,2048]{2,1,0:T(8,128)(2,1)} %subtract_convert_fusion, f32[1024]{0:T(1024)S(1)} %copy-done.8, s32[2048]{0:T(1024)S(1)} %iota_add_fusion, s32[1024]{0:T(1024)S(1)} %iota_add_fusion.1), kind=kOutput, calls=%fused_computation.20 | convolution fusion | flops 5377097728 | bytes 24657920 | tf_op jit(solution)/shard_map/dot_general | solution.py:111
  (215 shorter events, 99.6 us)
Async XLA Ops:
  3.4 6.0 %copy-start.9 = (bf16[640,128]{1,0:T(8,128)(2,1)S(1)}, bf16[640,128]{1,0:T(8,128)(2,1)}, u32[]{:S(2)}) copy-start(bf16[640,128]{1,0:T(8,128)(2,1)} %param.12) | copy-start | bytes 491524
  3.4 50.9 %copy-start.8 = (f32[1024]{0:T(1024)S(1)}, f32[1024]{0:T(1024)}, u32[]{:S(2)}) copy-start(f32[1024]{0:T(1024)} %param.14) | copy-start | bytes 12292
  4.7 57.7 %collective-permute-start.6 = (bf16[640,1024]{1,0:T(8,128)(2,1)}, bf16[640,1024]{1,0:T(8,128)(2,1)}, u32[]{:S(2)}, u32[]{:S(2)}) collective-permute-start(bf16[640,1024]{1,0:T(8,128)(2,1)} %slice.197), channel_id=1, source_target_pairs={{0,2},{4,6},{8,10},{12,14},{16,18},{20,22},{24,26},{28,30}} | collective-permute-start | bytes 3932168 | tf_op jit(solution)/shard_map/ppermute | solution.py:55
  6.4 54.2 %collective-permute-start.8 = (bf16[640,1024]{1,0:T(8,128)(2,1)}, bf16[640,1024]{1,0:T(8,128)(2,1)}, u32[]{:S(2)}, u32[]{:S(2)}) collective-permute-start(bf16[640,1024]{1,0:T(8,128)(2,1)} %slice.197), channel_id=1, source_target_pairs={{0,16},{4,20},{8,24},{12,28},{16,0},{20,4},{24,8},{28,12}} | collective-permute-start | bytes 3932168 | tf_op jit(solution)/shard_map/ppermute | solution.py:34
  8.1 63.4 %collective-permute-start.2 = (bf16[640,2048]{1,0:T(8,128)(2,1)S(1)}, bf16[640,2048]{1,0:T(8,128)(2,1)}, u32[]{:S(2)}, u32[]{:S(2)}) collective-permute-start(bf16[640,2048]{1,0:T(8,128)(2,1)S(1)} %broadcast_select_fusion.3), channel_id=1, source_target_pairs={{0,16},{1,17},{2,18},{3,19},{4,20},{5,21},{6,22},{7,23},{8,24},{9,... | collective-permute-start | bytes 7864328 | tf_op jit(solution)/shard_map/ppermute | solution.py:34
  54.0 16.8 %collective-permute-start.5 = (bf16[2,128,320]{1,2,0:T(8,128)(2,1)S(1)}, bf16[2,128,320]{1,2,0:T(8,128)(2,1)S(1)}, u32[]{:S(2)}, u32[]{:S(2)}) collective-permute-start(bf16[2,128,320]{1,2,0:T(8,128)(2,1)S(1)} %convolution_convert_fusion.3), channel_id=1, source_target_pairs={{0,16},{1,17},{2,18},{3,19},{4,20},{5,21},{6,22},{7,23},{8,24},{9,... | collective-permute-start | bytes 491528 | tf_op jit(solution)/shard_map/ppermute | solution.py:34
  54.3 6.1 %collective-permute-start.11 = (f32[1024]{0:T(1024)S(1)}, f32[1024]{0:T(1024)S(1)}, u32[]{:S(2)}, u32[]{:S(2)}) collective-permute-start(f32[1024]{0:T(1024)S(1)} %copy-done.8), channel_id=1, source_target_pairs={{0,4},{1,5},{2,6},{3,7},{4,0},{5,1},{6,2},{7,3},{8,12},{9,13},{10,... | collective-permute-start | bytes 12296 | tf_op jit(solution)/shard_map/ppermute | solution.py:79
  60.5 8.7 %copy-start.17 = (s32[8]{0:T(128)S(1)}, s32[8]{0:T(128)}, u32[]{:S(2)}) copy-start(s32[8]{0:T(128)} %constant.257.clone) | copy-start | bytes 100
  60.5 5.4 collective-permute-start.12
  60.6 16.0 %collective-permute-start.9 = (bf16[640,1024]{1,0:T(8,128)(2,1)}, bf16[640,1024]{1,0:T(8,128)(2,1)}, u32[]{:S(2)}, u32[]{:S(2)}) collective-permute-start(bf16[640,1024]{1,0:T(8,128)(2,1)} %collective-permute-done.8), channel_id=1, source_target_pairs={{0,2},{4,6},{8,10},{12,14},{16,18},{20,22},{24,26},{28,30}} | collective-permute-start | bytes 3932168 | tf_op jit(solution)/shard_map/ppermute | solution.py:55
  64.6 32.3 %collective-permute-start = (bf16[640,1024]{1,0:T(8,128)(2,1)}, bf16[640,1024]{1,0:T(8,128)(2,1)}, u32[]{:S(2)}, u32[]{:S(2)}) collective-permute-start(bf16[640,1024]{1,0:T(8,128)(2,1)} %get-tuple-element.48), channel_id=1, source_target_pairs={{0,2},{4,6},{9,11},{13,15},{18,16},{22,20},{27,25},{31,29}} | collective-permute-start | bytes 3932168 | tf_op jit(solution)/shard_map/ppermute | solution.py:55
  65.9 4.9 collective-permute-start.13
  70.8 86.7 %copy-start.15 = (f32[1024]{0:T(1024)}, f32[1024]{0:T(1024)S(1)}, u32[]{:S(2)}) copy-start(f32[1024]{0:T(1024)S(1)} %fusion.86) | copy-start | bytes 12292
  74.0 50.3 %collective-permute-start.3 = (bf16[640,1024]{1,0:T(8,128)(2,1)}, bf16[640,1024]{1,0:T(8,128)(2,1)}, u32[]{:S(2)}, u32[]{:S(2)}) collective-permute-start(bf16[640,1024]{1,0:T(8,128)(2,1)} %constant_dynamic-slice_fusion.2), channel_id=1, source_target_pairs={{0,2},{4,6},{9,11},{13,15},{18,16},{22,20},{27,25},{31,29}} | collective-permute-start | bytes 3932168 | tf_op jit(solution)/shard_map/ppermute | solution.py:55
  75.3 63.8 %collective-permute-start.7 = (bf16[640,1024]{1,0:T(8,128)(2,1)}, bf16[640,1024]{1,0:T(8,128)(2,1)}, u32[]{:S(2)}, u32[]{:S(2)}) collective-permute-start(bf16[640,1024]{1,0:T(8,128)(2,1)} %get-tuple-element.49), channel_id=1, source_target_pairs={{0,1},{2,3},{4,5},{6,7},{8,9},{10,11},{12,13},{14,15},{16,17},{18,... | collective-permute-start | bytes 3932168 | tf_op jit(solution)/shard_map/ppermute | solution.py:55
  79.2 30.1 %copy-start.5 = (bf16[1,640,2048]{2,1,0:T(8,128)(2,1)S(1)}, bf16[1,640,2048]{2,1,0:T(8,128)(2,1)}, u32[]{:S(2)}) copy-start(bf16[1,640,2048]{2,1,0:T(8,128)(2,1)} %fusion.130) | copy-start | bytes 7864324
  79.2 61.4 %collective-permute-start.10 = (bf16[640,1024]{1,0:T(8,128)(2,1)}, bf16[640,1024]{1,0:T(8,128)(2,1)}, u32[]{:S(2)}, u32[]{:S(2)}) collective-permute-start(bf16[640,1024]{1,0:T(8,128)(2,1)} %broadcast_select_fusion.6), channel_id=1, source_target_pairs={{0,1},{2,3},{4,5},{6,7},{8,9},{10,11},{12,13},{14,15},{16,17},{18,... | collective-permute-start | bytes 3932168 | tf_op jit(solution)/shard_map/ppermute | solution.py:55
  99.5 45.1 %collective-permute-start.1 = (bf16[640,1024]{1,0:T(8,128)(2,1)}, bf16[640,1024]{1,0:T(8,128)(2,1)}, u32[]{:S(2)}, u32[]{:S(2)}) collective-permute-start(bf16[640,1024]{1,0:T(8,128)(2,1)} %broadcast_select_fusion.9), channel_id=1, source_target_pairs={{0,1},{2,3},{4,5},{6,7},{9,8},{11,10},{13,12},{15,14},{18,19},{16,... | collective-permute-start | bytes 3932168 | tf_op jit(solution)/shard_map/ppermute | solution.py:55
  127.5 18.5 %collective-permute-start.4 = (bf16[640,1024]{1,0:T(8,128)(2,1)}, bf16[640,1024]{1,0:T(8,128)(2,1)}, u32[]{:S(2)}, u32[]{:S(2)}) collective-permute-start(bf16[640,1024]{1,0:T(8,128)(2,1)} %broadcast_select_fusion.8), channel_id=1, source_target_pairs={{0,1},{2,3},{4,5},{6,7},{9,8},{11,10},{13,12},{15,14},{18,19},{16,... | collective-permute-start | bytes 3932168 | tf_op jit(solution)/shard_map/ppermute | solution.py:55
  163.0 2.3 copy-start.6
  258.4 39.8 %copy-start.7 = (f32[512,512]{1,0:T(8,128)}, f32[512,512]{1,0:T(8,128)S(1)}, u32[]{:S(2)}) copy-start(f32[512,512]{1,0:T(8,128)S(1)} %get-tuple-element.173) | copy-start | bytes 3145732
  258.4 43.8 %copy-start.10 = (s32[4,2]{0,1:T(2,128)}, s32[4,2]{0,1:T(2,128)S(1)}, u32[]{:S(2)}) copy-start(s32[4,2]{0,1:T(2,128)S(1)} %get-tuple-element.178) | copy-start | bytes 100
  298.2 4.0 copy-start.14
  298.2 4.0 copy-start.16
  302.2 13.7 %copy-start.3 = (bf16[4,320,1024]{2,1,0:T(8,128)(2,1)}, bf16[4,320,1024]{2,1,0:T(8,128)(2,1)S(1)}, u32[]{:S(2)}) copy-start(bf16[4,320,1024]{2,1,0:T(8,128)(2,1)S(1)} %subtract_convert_fusion.2) | copy-start | bytes 7864324
  315.9 6.5 %copy-start.1 = (f32[1024,3072]{1,0:T(8,128)}, f32[1024,3072]{1,0:T(8,128)S(1)}, u32[]{:S(2)}) copy-start(f32[1024,3072]{1,0:T(8,128)S(1)} %select_add_fusion) | copy-start | bytes 37748740
  322.3 5.2 slice-start
  324.1 3.5 slice-start.1
  343.0 4.7 slice-start.6
  343.0 4.7 slice-start.7
  343.5 3.5 copy-start.13
  347.0 2.2 slice-start.8
  349.2 12.9 %copy-start = (f32[512,3072]{1,0:T(8,128)}, f32[512,3072]{1,0:T(8,128)S(1)}, u32[]{:S(2)}) copy-start(f32[512,3072]{1,0:T(8,128)S(1)} %slice_select_fusion) | copy-start | bytes 18874372
  387.0 61.8 %copy-start.11 = (s32[4,2]{0,1:T(2,128)S(1)}, s32[4,2]{0,1:T(2,128)}, u32[]{:S(2)}) copy-start(s32[4,2]{0,1:T(2,128)} %copy-done.10) | copy-start | bytes 100
  499.6 6.4 %slice-start.4 = ((s8[6291456]{0:T(1024)(128)(4,1)}), s8[4194304]{0:T(1024)(128)(4,1)S(1)}, s32[]{:S(2)}) async-start(s8[6291456]{0:T(1024)(128)(4,1)} %bitcast.164), calls=%async_computation.4 | async-start | bytes 8388608
  501.0 4.9 slice-start.5
  510.4 1.5 copy-start.12
  510.4 3.2 slice-start.2
  512.0 1.8 slice-start.3
  513.7 31.4 %copy-start.2 = (f32[1,2048,512]{1,2,0:T(8,128)S(1)}, f32[1,2048,512]{1,2,0:T(8,128)}, u32[]{:S(2)}) copy-start(f32[1,2048,512]{1,2,0:T(8,128)} %slice_bitcast_fusion.1) | copy-start | bytes 12582916
  549.4 8.8 %copy-start.4 = (bf16[4,320,1024]{2,1,0:T(8,128)(2,1)S(1)}, bf16[4,320,1024]{2,1,0:T(8,128)(2,1)}, u32[]{:S(2)}) copy-start(bf16[4,320,1024]{2,1,0:T(8,128)(2,1)} %copy-done.3) | copy-start | bytes 7864324
